TPU v7x, 512 devices: a whole 4x8x8 slice. The times are simulated.
512 devices in a mesh: section: 16 (over y_hi, x, core), seq: 32 (over y_lo, z).
Axes of the slice: x: 4, y: 8 (y_hi: 2, y_lo: 4; y = y_hi * 4 + y_lo), z: 8, core: 2. Of those that a mesh axis runs over, the one named last changes fastest.
Arguments:
- hidden: bfloat16 [16, 512, 4096], P('section', 'seq'), may hold values from -6 to 6
- modulation: float32 [16, 3, 4096], P('section'), may hold values from -3 to 3
- w_qkv: bfloat16 [16, 4096, 3, 4096], P('section', None, None, 'seq'), may hold values from -0.09375 to 0.09375
- qk_gain: float32 [16, 2, 128], P('section'), may hold values from 1 to 2.5
- w_out: bfloat16 [16, 4096, 4096], P('section', 'seq'), may hold values from -0.1875 to 0.1875
- stale_kv: bfloat16 [16, 2, 1024, 4096], P('section', None, None, 'seq')
- patch_start: int32 [16], P('section'), may hold values from 0 to 512
Outputs:
- passed: bfloat16 [16, 512, 4096], P('section', 'seq')
All inputs are finite; a program needn't handle non-finite values.
Results may differ from a plain program's by a relative error of at most 0.024.
Values may be sent and summed in bfloat16 or wider, within the bound.
A program may use at most 64 MiB of HBM per device.

v0:
```python
import math

import jax
import jax.numpy as jnp
from jax import lax
from jax.sharding import PartitionSpec as P


def from_behind(block, axis, distance):
    devices = range(lax.axis_size(axis))
    route = [((i - distance) % len(devices), i) for i in devices]
    return lax.ppermute(block, axis, route)


def modulate(tokens_in, modulation):
    values = tokens_in.astype(jnp.float32)
    average = jnp.mean(values, axis=-1, keepdims=True)
    centred = values - average
    spread = jnp.mean(centred * centred, axis=-1, keepdims=True)
    normed = centred * lax.rsqrt(spread + 1e-06)
    return (values, (normed * (1.0 + modulation[1]) + modulation[0]).astype(jnp.bfloat16))


def head_norm(values, gains):
    return values * lax.rsqrt(jnp.mean(values * values, axis=-1, keepdims=True) + 1e-06) * gains


def per_device(hidden, modulation, w_qkv, qk_gain, w_out, stale_kv, patch_start):
    tokens_in = hidden[0]
    own_rows = tokens_in.shape[0]
    width = w_qkv.shape[1]
    head_size = w_qkv.shape[3]
    layer_mod = modulation[0]
    values, mixed = modulate(tokens_in, layer_mod)
    projection = w_qkv[0].reshape(width, 3 * head_size)
    merged = jnp.dot(
        lax.all_gather(mixed, "seq", axis=0, tiled=True),
        projection,
        preferred_element_type=jnp.float32,
    )
    patch_rows = merged.shape[0]
    merged = merged.reshape(patch_rows, 3, head_size)
    queries = head_norm(merged[:, 0], qk_gain[0, 0]).astype(jnp.bfloat16)
    keys_new = head_norm(merged[:, 1], qk_gain[0, 1]).astype(jnp.bfloat16)
    values_new = merged[:, 2].astype(jnp.bfloat16)
    anchor = patch_start[0]
    stale_keys = stale_kv[0, 0]
    stale_values = stale_kv[0, 1]
    scaling = 1.0 / math.sqrt(head_size)
    nought = jnp.zeros((), jnp.int32)
    keys_all = lax.dynamic_update_slice(stale_keys, keys_new, (anchor, nought))
    values_all = lax.dynamic_update_slice(stale_values, values_new, (anchor, nought))
    scores = jnp.dot(queries, keys_all.T, preferred_element_type=jnp.float32) * scaling
    highest = jnp.max(scores, axis=-1, keepdims=True)
    raised = jnp.exp(scores - highest)
    probs = (raised / jnp.sum(raised, axis=-1, keepdims=True)).astype(jnp.bfloat16)
    attended = jnp.dot(probs, values_all, preferred_element_type=jnp.float32).astype(jnp.bfloat16)
    out_weight = w_out[0]
    partial_value = jnp.dot(attended, out_weight, preferred_element_type=jnp.float32)
    summed = lax.psum(partial_value.astype(jnp.bfloat16), "seq").astype(jnp.float32)
    running = lax.dynamic_slice_in_dim(summed, lax.axis_index("seq") * own_rows, own_rows, 0)
    layer_out = (values + layer_mod[2] * running).astype(jnp.bfloat16)
    received = from_behind(layer_out, "section", 1)
    return received[None]


def solution(mesh):
    in_specs = (
        P("section", "seq", None),
        P("section", None, None),
        P("section", None, None, "seq"),
        P("section", None, None),
        P("section", "seq", None),
        P("section", None, None, "seq"),
        P("section"),
    )
    out_specs = P("section", "seq", None)
    return jax.shard_map(
        per_device, mesh=mesh, in_specs=in_specs, out_specs=out_specs, check_vma=False
    )
```

profile of v0, /device:TPU:1, one launch (start us, length us, event | category | flops | bytes accessed | tf_op | source)
XLA Modules:
  0.0 524.0 jit_solution(13584433727402125432)
XLA Ops:
  6.5 0.9 fusion.24
  7.4 1.0 convert_reduce_fusion
  8.5 1.1 fusion.13
  9.6 1.7 fusion.16
  11.3 0.0 all-gather.2.cloned.1.call-update
  11.3 0.0 copy-start.6
  11.3 0.0 copy-start.3
  11.3 0.0 all-reduce.2.cloned.1.call-start
  11.4 4.8 copy.10
  16.8 0.6 slice_bitcast_fusion.5
  17.4 0.7 slice_bitcast_fusion.3
  18.1 139.4 %all-gather.2.cloned.1.call-done = bf16[512,4096]{1,0:T(8,128)(2,1)} async-done(((bf16[16,4096]{1,0:T(8,128)(2,1)}), bf16[512,4096]{1,0:T(8,128)(2,1)}) %all-gather.2.cloned.1.call-update) | async-done | bytes 4194320 | tf_op jit(solution)/shard_map/all_gather | solution.py:37
  157.5 5.0 fusion
  162.5 0.0 copy-start.2
  162.5 0.1 multiply_reduce_fusion.2
  162.6 0.7 add_rsqrt_fusion
  163.3 0.1 copy-done.2
  163.4 0.1 multiply_convert_fusion
  163.5 0.1 copy.11
  163.6 0.1 copy.12
  163.7 0.5 dynamic_update_slice.6
  164.2 1.6 multiply_reduce_fusion
  165.8 1.1 fusion.3
  166.9 0.0 copy-done.5
  166.9 0.4 dynamic_update_slice.7
  167.3 4.1 convolution_convert_fusion
  171.5 0.0 all-reduce.2.cloned.1.call-update
  171.5 316.3 %all-reduce.2.cloned.1.call-done = bf16[512,4096]{1,0:T(8,128)(2,1)} async-done(((bf16[512,4096]{1,0:T(8,128)(2,1)}), bf16[512,4096]{1,0:T(8,128)(2,1)}) %all-reduce.2.cloned.1.call-update) | async-done | bytes 4194320 | tf_op jit(solution)/shard_map/psum | solution.py:60
  487.8 0.9 fusion.17
  488.8 25.8 %collective-permute-start = (bf16[16,4096]{1,0:T(8,128)(2,1)S(1)}, bf16[16,4096]{1,0:T(8,128)(2,1)S(1)}, u32[]{:S(2)}, u32[]{:S(2)}) collective-permute-start(bf16[16,4096]{1,0:T(8,128)(2,1)S(1)} %fusion.17), channel_id=1, source_target_pairs={{480,0},{0,32},{32,64},{64,96},{96,128},{128,160},{160,192},{192,2... | collective-permute-start | bytes 393224 | tf_op jit(solution)/shard_map/ppermute | solution.py:12
  514.5 1.9 collective-permute-done
  516.5 0.7 copy.18
  (13 shorter events, 0.1 us)
Async XLA Ops:
  6.5 160.8 %copy-start = (bf16[1,128,4096]{2,1,0:T(8,128)(2,1)S(1)}, bf16[1,128,4096]{2,1,0:T(8,128)(2,1)}, u32[]{:S(2)}) copy-start(bf16[1,128,4096]{2,1,0:T(8,128)(2,1)} %param.11) | copy-start | bytes 3145732
  6.5 151.0 %all-gather.2.cloned.1.call-start = ((), (), s32[]{:S(2)}) async-start(), calls=%async_computation | async-start | bytes 4325376 | tf_op jit(solution)/shard_map/all_gather | solution.py:37
  11.3 5.5 %copy-start.6 = (f32[1,2,128]{2,1,0:T(2,128)S(1)}, f32[1,2,128]{2,1,0:T(2,128)}, u32[]{:S(2)}) copy-start(f32[1,2,128]{2,1,0:T(2,128)} %param.10) | copy-start | bytes 3076
  11.3 6.1 %copy-start.3 = (bf16[1,2,1024,128]{3,2,1,0:T(8,128)(2,1)S(1)}, bf16[1,2,1024,128]{3,2,1,0:T(8,128)(2,1)}, u32[]{:S(2)}) copy-start(bf16[1,2,1024,128]{3,2,1,0:T(8,128)(2,1)} %param.12) | copy-start | bytes 1572868
  11.3 476.5 %all-reduce.2.cloned.1.call-start = ((), (), s32[]{:S(2)}) async-start(), calls=%async_computation.1 | async-start | bytes 8388608 | tf_op jit(solution)/shard_map/psum | solution.py:60
  162.5 0.9 copy-start.2
  165.8 1.1 copy-start.5
  165.8 1.1 copy-start.4
  171.5 316.4 %copy-start.1 = (bf16[1,16,4096]{2,1,0:T(8,128)(2,1)S(1)}, bf16[1,16,4096]{2,1,0:T(8,128)(2,1)}, u32[]{:S(2)}) copy-start(bf16[1,16,4096]{2,1,0:T(8,128)(2,1)} %param.7) | copy-start | bytes 393220
  488.8 27.7 %collective-permute-start = (bf16[16,4096]{1,0:T(8,128)(2,1)S(1)}, bf16[16,4096]{1,0:T(8,128)(2,1)S(1)}, u32[]{:S(2)}, u32[]{:S(2)}) collective-permute-start(bf16[16,4096]{1,0:T(8,128)(2,1)S(1)} %fusion.17), channel_id=1, source_target_pairs={{480,0},{0,32},{32,64},{64,96},{96,128},{128,160},{160,192},{192,2... | collective-permute-start | bytes 393224 | tf_op jit(solution)/shard_map/ppermute | solution.py:12
Sparse Core Ops, SparseCore 0:
  11.4 146.0 all-gather.1
  171.6 316.1 all-reduce.1
where the time goes:
time: 529 us; the launch traced here: 524 us
  waiting for transfers between devices  458 us (87%)
  starting transfers between devices  25.8 us (5%)
  between operations  14.2 us (3%)
  matrix products  10.7 us (2%)
  local copies, waits for them, and re-layouts  8.01 us (2%)
  other arithmetic  7.6 us (1%)
    psum x1, waiting for transfers between devices, per_device(): lax.psum(partial_value.astype(jnp.bfloat16), 'seq').astype(jnp.float32)  316 us
    all_gather x1, waiting for transfers between devices, per_device(): lax.all_gather(mixed, 'seq', axis=0, tiled=True)  139 us
    ppermute x1, starting transfers between devices, from_behind(): return lax.ppermute(block, axis, route)  25.8 us
  transfers between devices with their start and end apart: 3, of which 3 were waited for; matrix products, arithmetic and copies ran while one was open for 1% of the time, Pallas kernels for 0%

commit v1 on v0

v1 whole, which is shorter than its diff:
```python
import functools
import math

import jax
import jax.numpy as jnp
from jax import lax
from jax.experimental import pallas as pl
from jax.experimental.pallas import tpu as pltpu
from jax.sharding import PartitionSpec as P

MESH = pl.DeviceIdType.MESH
NY = 4
NZ = 8
PEERS = (1, 3, 2)
ORDER = (4, 3, -3, 2, -2, 1, -1, 0)


def kernel(
    sections,
    hid,
    mod,
    wq_hbm,
    gain,
    wo_hbm,
    st_hbm,
    start,
    out,
    rows_all,
    w_all,
    w_cols,
    stale,
    keys,
    vals,
    queries,
    heads,
    part_out,
    part_in,
    hid_cols,
    out_rows,
    local_sem,
    y_send,
    y_recv,
    hid_send,
    hid_recv,
    w_send,
    w_recv,
    z_send,
    z_recv,
    head_send,
    head_recv,
    ring_send,
    ring_recv,
    out_send,
    out_recv,
):
    own, width = hid.shape
    head_size = gain.shape[1]
    block = NY * own
    half = block // 2
    cols = width // NY
    patch = block * NZ
    section = lax.axis_index("section")
    place = lax.axis_index("seq")
    y = place // NZ
    z = place % NZ
    after = (section + 1) % sections
    before = (section + sections - 1) % sections

    def y_at(distance):
        return (y + distance + NY) % NY

    def z_at(distance):
        return (z + distance + NZ) % NZ

    def remote(src, dst, send, recv, yy, zz, sec=section):
        return pltpu.make_async_remote_copy(
            src_ref=src,
            dst_ref=dst,
            send_sem=send,
            recv_sem=recv,
            device_id=(sec, yy * NZ + zz),
            device_id_type=MESH,
        )

    local = [
        pltpu.make_async_copy(
            wq_hbm.at[j], w_all.at[:, pl.ds(j * head_size, head_size)], local_sem.at[j]
        )
        for j in range(3)
    ]
    local.append(pltpu.make_async_copy(st_hbm, stale, local_sem.at[3]))
    my_cols = pl.ds(pl.multiple_of(y * cols, cols), cols)
    local.append(
        pltpu.make_async_copy(wo_hbm.at[:, my_cols], w_cols.at[y], local_sem.at[4])
    )
    for copy in local:
        copy.start()

    barrier = pltpu.get_barrier_semaphore()
    partners = [(section, y_at(e) * NZ + z) for e in PEERS]
    partners += [(section, y * NZ + z_at(s)) for s in (1, -1)]
    partners += [(after, yy * NZ + z) for yy in range(NY)]
    partners += [(before, yy * NZ + z) for yy in range(NY)]
    for partner in partners:
        pl.semaphore_signal(barrier, inc=1, device_id=partner, device_id_type=MESH)

    values = hid[...].astype(jnp.float32)
    average = jnp.mean(values, axis=-1, keepdims=True)
    centred = values - average
    spread = jnp.mean(centred * centred, axis=-1, keepdims=True)
    normed = centred * lax.rsqrt(spread + 1e-06)
    mixed = normed * (1.0 + mod[1:2, :]) + mod[0:1, :]
    rows_all[z, y] = mixed.astype(jnp.bfloat16)
    hid_cols[y] = hid[:, my_cols]

    pl.semaphore_wait(barrier, len(partners))

    def y_copy(e):
        mine = rows_all.at[z, y]
        return remote(mine, mine, y_send.at[e], y_recv.at[e], y_at(e), z)

    def y_wait(e):
        slot = rows_all.at[z, y_at(-e)]
        remote(slot, slot, y_send.at[e], y_recv.at[e], y_at(e), z).wait_recv()

    def z_copy(way, h, e):
        s = 1 - 2 * way
        slot = rows_all.at[z_at(-s * h), y_at(-e)]
        return remote(
            slot, slot, z_send.at[way, h, e], z_recv.at[way, h, e], y, z_at(s)
        )

    def z_wait(way, h, e):
        s = 1 - 2 * way
        slot = rows_all.at[z_at(-s * (h + 1)), y_at(-e)]
        remote(
            slot, slot, z_send.at[way, h, e], z_recv.at[way, h, e], y, z_at(s)
        ).wait_recv()

    def far(way, e):
        return (e % 2) == way

    def hid_copy(e):
        there = pl.ds(pl.multiple_of(y_at(e) * cols, cols), cols)
        return remote(
            hid.at[:, there], hid_cols.at[y], hid_send.at[e], hid_recv.at[e], y_at(e), z
        )

    def w_copy(e):
        there = pl.ds(pl.multiple_of(y_at(e) * cols, cols), cols)
        return remote(
            wo_hbm.at[:, there], w_cols.at[y], w_send.at[e], w_recv.at[e], y_at(e), z
        )

    for e in PEERS:
        y_copy(e).start()
    for way in range(2):
        z_copy(way, 0, 0).start()
    for e in PEERS:
        hid_copy(e).start()
    for e in PEERS:
        w_copy(e).start()
    for e in PEERS:
        y_wait(e)
        for way in range(2):
            z_copy(way, 0, e).start()

    local[3].wait()
    first = start[0]
    row = lax.broadcasted_iota(jnp.int32, (patch, head_size), 0)
    for j, target in ((0, keys), (1, vals)):
        low = stale[j, pl.ds(0, patch), :].astype(jnp.float32)
        high = stale[j, pl.ds(patch, patch), :].astype(jnp.float32)
        target[pl.ds(0, patch), :] = jnp.where(row < first, low, high).astype(
            jnp.bfloat16
        )
    for j in range(3):
        local[j].wait()

    query_scale = math.log2(math.e) / math.sqrt(head_size)

    def project(places):
        pieces = [rows_all[at].reshape(block, width) for at in places]
        merged = jnp.dot(
            pieces[0] if len(pieces) == 1 else jnp.concatenate(pieces, axis=0),
            w_all[...],
            preferred_element_type=jnp.float32,
        )
        q = merged[:, :head_size]
        k = merged[:, head_size : 2 * head_size]
        v = merged[:, 2 * head_size :].astype(jnp.bfloat16)
        q = q * lax.rsqrt(jnp.mean(q * q, axis=-1, keepdims=True) + 1e-06)
        q = (q * (gain[0:1, :] * query_scale)).astype(jnp.bfloat16)
        k = k * lax.rsqrt(jnp.mean(k * k, axis=-1, keepdims=True) + 1e-06)
        k = (k * gain[1:2, :]).astype(jnp.bfloat16)
        for i, at in enumerate(places):
            here = slice(i * block, (i + 1) * block)
            there = pl.ds(pl.multiple_of(patch + at * block, block), block)
            queries[at] = q[here]
            keys[there, :] = k[here]
            vals[there, :] = v[here]

    project([z])

    def hop(h, carry):
        for e in (0, *PEERS):
            for way in range(2):
                z_wait(way, h - 1, e)
                if far(way, e):
                    z_copy(way, h, e).start()
                else:

                    @pl.when(h < 3)
                    def _():
                        z_copy(way, h, e).start()

        project([z_at(-h), z_at(h)])
        return carry

    lax.fori_loop(1, 4, hop, 0)
    for e in (0, *PEERS):
        z_wait(e % 2, 3, e)
    project([z_at(4)])

    def head_copy(i, e):
        mine = heads.at[z_at(ORDER[i]), y]
        return remote(mine, mine, head_send.at[i, e], head_recv.at[i, e], y_at(e), z)

    def attend(i):
        at = z_at(ORDER[i])
        scores = lax.dot_general(
            queries[at],
            keys[...],
            (((1,), (1,)), ((), ())),
            preferred_element_type=jnp.float32,
        )
        highest = jnp.max(scores, axis=-1, keepdims=True)
        raised = jnp.exp2(scores - highest)
        total = jnp.sum(raised, axis=-1, keepdims=True)
        mixed_values = jnp.dot(
            raised.astype(jnp.bfloat16), vals[...], preferred_element_type=jnp.float32
        )
        heads[at, y] = (mixed_values / total).astype(jnp.bfloat16)
        for e in PEERS:
            head_copy(i, e).start()

    def ring_copy(way, part, k):
        return remote(
            part_out.at[way, part, k - 1],
            part_in.at[way, part, k - 1],
            ring_send.at[way, part, k - 1],
            ring_recv.at[way, part, k - 1],
            y,
            z_at(1 - 2 * way),
        )

    def length(way, part):
        return 4 if way == part else 3

    def finish(i):
        offset = ORDER[i]
        at = z_at(offset)
        for e in PEERS:
            slot = heads.at[at, y_at(-e)]
            remote(
                slot, slot, head_send.at[i, e], head_recv.at[i, e], y_at(e), z
            ).wait_recv()
        four = jnp.concatenate([heads[at, yy] for yy in range(NY)], axis=1)
        summed = jnp.dot(
            four,
            w_cols[...].reshape(NY * head_size, cols),
            preferred_element_type=jnp.float32,
        )
        pieces = [summed[:half], summed[half:]]
        k = abs(offset)
        ways = (0, 1) if k in (0, 4) else ((0,) if offset > 0 else (1,))
        for way in ways:
            for part in range(2):
                if k > length(way, part):
                    continue
                if k < length(way, part):
                    ring_copy(way, part, k + 1).wait_recv()
                    added = pieces[part] + part_in[way, part, k].astype(jnp.float32)
                else:
                    added = pieces[part]
                if k > 0:
                    part_out[way, part, k - 1] = added.astype(jnp.bfloat16)
                    ring_copy(way, part, k).start()
                else:
                    pieces[part] = added
        return pieces

    blocks = len(ORDER)
    ahead = 2
    pieces = None
    for i in range(blocks + ahead):
        if i < blocks:
            attend(i)
        if i == ahead:
            for e in PEERS:
                slot = w_cols.at[y_at(-e)]
                remote(slot, slot, w_send.at[e], w_recv.at[e], y_at(e), z).wait_recv()
                slot = hid_cols.at[y_at(-e)]
                remote(
                    slot, slot, hid_send.at[e], hid_recv.at[e], y_at(e), z
                ).wait_recv()
            local[4].wait()
        if i >= ahead:
            pieces = finish(i - ahead)

    def out_copy(yy):
        return remote(
            out_rows.at[yy],
            out.at[:, my_cols],
            out_send.at[yy],
            out_recv.at[y],
            yy,
            z,
            after,
        )

    gate = mod[2:3, my_cols]
    for yy in range(NY):
        total = pieces[yy // 2][(yy % 2) * own : (yy % 2 + 1) * own]
        layer_out = hid_cols[yy].astype(jnp.float32) + gate * total
        out_rows[yy] = layer_out.astype(jnp.bfloat16)
        out_copy(yy).start()

    for e in PEERS:
        y_copy(e).wait_send()
        hid_copy(e).wait_send()
        w_copy(e).wait_send()
    for e in range(NY):
        for way in range(2):
            for h in range(4 if far(way, e) else 3):
                z_copy(way, h, e).wait_send()
    for i in range(blocks):
        for e in PEERS:
            head_copy(i, e).wait_send()
    for way in range(2):
        for part in range(2):
            for k in range(1, length(way, part) + 1):
                ring_copy(way, part, k).wait_send()
    for yy in range(NY):
        out_copy(yy).wait_send()
    for yy in range(NY):
        slot = out.at[:, pl.ds(yy * cols, cols)]
        remote(
            out_rows.at[yy], slot, out_send.at[yy], out_recv.at[yy], yy, z, after
        ).wait_recv()


def per_device(sections, hidden, modulation, w_qkv, qk_gain, w_out, stale_kv, patch_start):
    own, width = hidden.shape[1:]
    head_size = qk_gain.shape[2]
    clip = stale_kv.shape[2]
    block = NY * own
    cols = width // NY
    bf16 = jnp.bfloat16
    dma = pltpu.SemaphoreType.DMA
    vmem = pl.BlockSpec(memory_space=pltpu.VMEM)
    anywhere = pl.BlockSpec(memory_space=pl.ANY)
    smem = pl.BlockSpec(memory_space=pltpu.SMEM)
    received = pl.pallas_call(
        functools.partial(kernel, sections),
        out_shape=jax.ShapeDtypeStruct((own, width), bf16),
        in_specs=[vmem, vmem, anywhere, vmem, anywhere, anywhere, smem],
        out_specs=vmem,
        scratch_shapes=[
            pltpu.VMEM((NZ, NY, own, width), bf16),
            pltpu.VMEM((width, 3 * head_size), bf16),
            pltpu.VMEM((NY, head_size, cols), bf16),
            pltpu.VMEM((2, clip, head_size), bf16),
            pltpu.VMEM((clip, head_size), bf16),
            pltpu.VMEM((clip, head_size), bf16),
            pltpu.VMEM((NZ, block, head_size), bf16),
            pltpu.VMEM((NZ, NY, block, head_size), bf16),
            pltpu.VMEM((2, 2, 4, block // 2, cols), bf16),
            pltpu.VMEM((2, 2, 4, block // 2, cols), bf16),
            pltpu.VMEM((NY, own, cols), bf16),
            pltpu.VMEM((NY, own, cols), bf16),
            dma((5,)),
            dma((NY,)),
            dma((NY,)),
            dma((NY,)),
            dma((NY,)),
            dma((NY,)),
            dma((NY,)),
            dma((2, 4, NY)),
            dma((2, 4, NY)),
            dma((NZ, NY)),
            dma((NZ, NY)),
            dma((2, 2, 4)),
            dma((2, 2, 4)),
            dma((NY,)),
            dma((NY,)),
        ],
        compiler_params=pltpu.CompilerParams(
            collective_id=0, has_side_effects=True, vmem_limit_bytes=48 << 20
        ),
    )(
        hidden[0],
        modulation[0],
        jnp.transpose(w_qkv[0], (1, 0, 2)),
        qk_gain[0],
        w_out[0],
        stale_kv[0],
        patch_start,
    )
    return received[None]


def solution(mesh):
    in_specs = (
        P("section", "seq", None),
        P("section", None, None),
        P("section", None, None, "seq"),
        P("section", None, None),
        P("section", "seq", None),
        P("section", None, None, "seq"),
        P("section"),
    )
    out_specs = P("section", "seq", None)
    return jax.shard_map(
        functools.partial(per_device, mesh.shape["section"]),
        mesh=mesh,
        in_specs=in_specs,
        out_specs=out_specs,
        check_vma=False,
    )
```

time: 529 us -> 103 us (0.19)
  the two profiles are of different devices: /device:TPU:1 before, /device:TPU:3 now
where the time goes in v1:
time: 103 us
  Pallas kernels  94.8 us (92%)
  local copies, waits for them, and re-layouts  7.23 us (7%)
    pallas_call x1, Pallas kernels, per_device(): pl.pallas_call(functools.partial(kernel, sections), out_shape=jax.ShapeDt...  94.8 us
    unnamed x12, local copies, waits for them, and re-layouts  7.23 us

profile of v1, /device:TPU:3, one launch (start us, length us, event | category | flops | bytes accessed | tf_op | source)
XLA Modules:
  0.0 102.7 jit_solution(15428193705652251822)
XLA Ops:
  0.7 0.8 copy.10
  1.5 0.0 copy-start
  1.5 1.9 %copy-done = bf16[1,4096,3,128]{3,1,2,0:T(8,128)(2,1)S(1)} copy-done((bf16[1,4096,3,128]{3,1,2,0:T(8,128)(2,1)S(1)}, bf16[1,4096,3,128]{3,1,2,0:T(8,128)(2,1)}, u32[]{:S(2)}) %copy-start) | copy-done | bytes 3145752
  3.4 0.0 copy-start.1
  3.4 1.2 %copy-done.1 = bf16[1,128,4096]{2,1,0:T(8,128)(2,1)S(1)} copy-done((bf16[1,128,4096]{2,1,0:T(8,128)(2,1)S(1)}, bf16[1,128,4096]{2,1,0:T(8,128)(2,1)}, u32[]{:S(2)}) %copy-start.1) | copy-done | bytes 1048600
  4.6 0.0 copy-start.2
  4.6 1.0 %copy-done.2 = bf16[1,2,1024,128]{3,2,1,0:T(8,128)(2,1)S(1)} copy-done((bf16[1,2,1024,128]{3,2,1,0:T(8,128)(2,1)S(1)}, bf16[1,2,1024,128]{3,2,1,0:T(8,128)(2,1)}, u32[]{:S(2)}) %copy-start.2) | copy-done | bytes 524312
  5.7 0.0 copy-start.3
  5.7 0.9 copy-done.3
  6.6 0.0 copy-start.4
  6.6 0.7 copy-done.4
  7.2 94.8 %shard_map.73 = bf16[16,4096]{1,0:T(8,128)(2,1)S(1)} custom-call(bf16[16,4096]{1,0:T(8,128)(2,1)S(1)} %bitcast.16, f32[3,4096]{1,0:T(4,128)S(1)} %bitcast.15, bf16[3,4096,128]{2,1,0:T(8,128)(2,1)S(1)} %bitcast.11, f32[2,128]{1,0:T(2,128)S(1)} %bitcast.17, bf16[128,4096]{1,0:T(8,128)(2,1)S(1)} %bitcast.12, bf16[2,1024,128]{2,1,0:T(8,128)(2,1)S(1)} %bitcast.13, ...), custom_call_target="tpu_custom_call" | custom-call | tf_op jit(solution)/shard_map/pallas_call | solution.py:364
  102.0 0.7 copy.13
Async XLA Ops:
  1.5 1.9 %copy-start = (bf16[1,4096,3,128]{3,1,2,0:T(8,128)(2,1)S(1)}, bf16[1,4096,3,128]{3,1,2,0:T(8,128)(2,1)}, u32[]{:S(2)}) copy-start(bf16[1,4096,3,128]{3,1,2,0:T(8,128)(2,1)} %param.9) | copy-start | bytes 9437188
  3.4 1.2 %copy-start.1 = (bf16[1,128,4096]{2,1,0:T(8,128)(2,1)S(1)}, bf16[1,128,4096]{2,1,0:T(8,128)(2,1)}, u32[]{:S(2)}) copy-start(bf16[1,128,4096]{2,1,0:T(8,128)(2,1)} %param.11) | copy-start | bytes 3145732
  4.6 1.0 %copy-start.2 = (bf16[1,2,1024,128]{3,2,1,0:T(8,128)(2,1)S(1)}, bf16[1,2,1024,128]{3,2,1,0:T(8,128)(2,1)}, u32[]{:S(2)}) copy-start(bf16[1,2,1024,128]{3,2,1,0:T(8,128)(2,1)} %param.12) | copy-start | bytes 1572868
  5.7 0.9 copy-start.3
  6.6 0.7 copy-start.4

commit v2 on v1

--- a/solution.py
+++ b/solution.py
@@ -13,18 +13,35 @@
 NZ = 8
 PEERS = (1, 3, 2)
 ORDER = (4, 3, -3, 2, -2, 1, -1, 0)
+PARTS = 2
+ARRIVALS = (
+    (1, 0, 0, 0), (0, 0, 1, 0), (0, 0, 1, 1), (3, 0, 0, 0), (0, 1, 1, 0), (0, 1, 1, 1),
+    (2, 0, 0, 0), (1, 0, 1, 0), (1, 0, 1, 1), (1, 1, 0, 0), (0, 0, 2, 0), (0, 0, 2, 1),
+    (3, 1, 0, 0), (3, 0, 1, 0), (3, 0, 1, 1), (0, 1, 2, 0), (0, 1, 2, 1), (2, 1, 0, 0),
+    (2, 0, 1, 0), (1, 0, 2, 0), (2, 0, 1, 1), (1, 0, 2, 1), (1, 1, 1, 0), (1, 1, 1, 1),
+    (0, 0, 3, 0), (0, 0, 3, 1), (3, 1, 1, 0), (3, 1, 1, 1), (3, 0, 2, 0), (3, 0, 2, 1),
+    (0, 1, 3, 0), (0, 1, 3, 1), (2, 1, 1, 0), (2, 1, 1, 1), (1, 0, 3, 0), (1, 0, 3, 1),
+    (2, 0, 2, 0), (2, 0, 2, 1), (1, 1, 2, 0), (1, 1, 2, 1), (0, 0, 4, 0), (3, 1, 2, 1),
+    (3, 0, 3, 1), (3, 1, 2, 0), (3, 0, 3, 0), (2, 1, 2, 1), (0, 1, 4, 0), (1, 0, 4, 1),
+    (2, 0, 3, 1), (2, 1, 2, 0), (1, 1, 3, 1), (2, 0, 3, 0), (1, 1, 3, 0), (3, 1, 3, 1),
+    (3, 0, 4, 1), (3, 1, 3, 0), (2, 1, 3, 0), (2, 1, 3, 1), (1, 1, 4, 1), (2, 0, 4, 0),
+    (3, 1, 4, 1), (2, 1, 4, 0),
+)
 
 
 def kernel(
     sections,
-    hid,
-    mod,
+    hid_hbm,
+    mod_hbm,
     wq_hbm,
-    gain,
+    gain_hbm,
     wo_hbm,
     st_hbm,
     start,
     out,
+    hid,
+    mod,
+    gain,
     rows_all,
     w_all,
     w_cols,
@@ -56,7 +73,6 @@
     own, width = hid.shape
     head_size = gain.shape[1]
     block = NY * own
-    half = block // 2
     cols = width // NY
     patch = block * NZ
     section = lax.axis_index("section")
@@ -66,11 +82,14 @@
     after = (section + 1) % sections
     before = (section + sections - 1) % sections
 
+    y_near = [(y + distance) % NY for distance in range(NY)]
+    z_near = [(z + distance) % NZ for distance in range(NZ)]
+
     def y_at(distance):
-        return (y + distance + NY) % NY
+        return y_near[distance % NY]
 
     def z_at(distance):
-        return (z + distance + NZ) % NZ
+        return z_near[distance % NZ]
 
     def remote(src, dst, send, recv, yy, zz, sec=section):
         return pltpu.make_async_remote_copy(
@@ -82,6 +101,14 @@
             device_id_type=MESH,
         )
 
+    first_local = [
+        pltpu.make_async_copy(src, dst, local_sem.at[5 + j])
+        for j, (src, dst) in enumerate(
+            ((hid_hbm, hid), (mod_hbm, mod), (gain_hbm, gain))
+        )
+    ]
+    for copy in first_local:
+        copy.start()
     local = [
         pltpu.make_async_copy(
             wq_hbm.at[j], w_all.at[:, pl.ds(j * head_size, head_size)], local_sem.at[j]
@@ -104,41 +131,46 @@
     for partner in partners:
         pl.semaphore_signal(barrier, inc=1, device_id=partner, device_id_type=MESH)
 
+    for copy in first_local:
+        copy.wait()
     values = hid[...].astype(jnp.float32)
     average = jnp.mean(values, axis=-1, keepdims=True)
     centred = values - average
     spread = jnp.mean(centred * centred, axis=-1, keepdims=True)
-    normed = centred * lax.rsqrt(spread + 1e-06)
-    mixed = normed * (1.0 + mod[1:2, :]) + mod[0:1, :]
-    rows_all[z, y] = mixed.astype(jnp.bfloat16)
-    hid_cols[y] = hid[:, my_cols]
-
+    scale = lax.rsqrt(spread + 1e-06)
+    piece = width // PARTS
+
+    def modulate(p):
+        here = slice(p * piece, (p + 1) * piece)
+        normed = centred[:, here] * scale
+        mixed = normed * (1.0 + mod[1, :, here]) + mod[0, :, here]
+        rows_all[z, p, y] = mixed.astype(jnp.bfloat16)
+
+    modulate(0)
     pl.semaphore_wait(barrier, len(partners))
 
-    def y_copy(e):
-        mine = rows_all.at[z, y]
-        return remote(mine, mine, y_send.at[e], y_recv.at[e], y_at(e), z)
-
-    def y_wait(e):
-        slot = rows_all.at[z, y_at(-e)]
-        remote(slot, slot, y_send.at[e], y_recv.at[e], y_at(e), z).wait_recv()
-
-    def z_copy(way, h, e):
+    def y_copy(e, p):
+        mine = rows_all.at[z, p, y]
+        return remote(mine, mine, y_send.at[e, p], y_recv.at[e, p], y_at(e), z)
+
+    def y_wait(e, p):
+        slot = rows_all.at[z, p, y_at(-e)]
+        remote(slot, slot, y_send.at[e, p], y_recv.at[e, p], y_at(e), z).wait_recv()
+
+    def z_copy(way, h, e, p):
         s = 1 - 2 * way
-        slot = rows_all.at[z_at(-s * h), y_at(-e)]
-        return remote(
-            slot, slot, z_send.at[way, h, e], z_recv.at[way, h, e], y, z_at(s)
-        )
-
-    def z_wait(way, h, e):
+        slot = rows_all.at[z_at(-s * h), p, y_at(-e)]
+        sems = (z_send.at[way, h, e, p], z_recv.at[way, h, e, p])
+        return remote(slot, slot, *sems, y, z_at(s))
+
+    def z_wait(way, h, e, p):
         s = 1 - 2 * way
-        slot = rows_all.at[z_at(-s * (h + 1)), y_at(-e)]
-        remote(
-            slot, slot, z_send.at[way, h, e], z_recv.at[way, h, e], y, z_at(s)
-        ).wait_recv()
-
-    def far(way, e):
-        return (e % 2) == way
+        slot = rows_all.at[z_at(-s * (h + 1)), p, y_at(-e)]
+        sems = (z_send.at[way, h, e, p], z_recv.at[way, h, e, p])
+        remote(slot, slot, *sems, y, z_at(s)).wait_recv()
+
+    def reach(way, e):
+        return 4 if (e % 2) == way else 3
 
     def hid_copy(e):
         there = pl.ds(pl.multiple_of(y_at(e) * cols, cols), cols)
@@ -152,18 +184,15 @@
             wo_hbm.at[:, there], w_cols.at[y], w_send.at[e], w_recv.at[e], y_at(e), z
         )
 
-    for e in PEERS:
-        y_copy(e).start()
-    for way in range(2):
-        z_copy(way, 0, 0).start()
-    for e in PEERS:
-        hid_copy(e).start()
-    for e in PEERS:
-        w_copy(e).start()
-    for e in PEERS:
-        y_wait(e)
+    for p in range(PARTS):
+        if p:
+            modulate(p)
         for way in range(2):
-            z_copy(way, 0, e).start()
+            z_copy(way, 0, 0, p).start()
+        if p == 0:
+            for e in PEERS:
+                y_copy(e, p).start()
+    hid_cols[y] = hid[:, my_cols]
 
     local[3].wait()
     first = start[0]
@@ -174,18 +203,17 @@
         target[pl.ds(0, patch), :] = jnp.where(row < first, low, high).astype(
             jnp.bfloat16
         )
-    for j in range(3):
-        local[j].wait()
-
     query_scale = math.log2(math.e) / math.sqrt(head_size)
 
     def project(places):
-        pieces = [rows_all[at].reshape(block, width) for at in places]
-        merged = jnp.dot(
-            pieces[0] if len(pieces) == 1 else jnp.concatenate(pieces, axis=0),
-            w_all[...],
-            preferred_element_type=jnp.float32,
-        )
+        merged = 0.0
+        for p in range(PARTS):
+            rows = [rows_all[at, p].reshape(block, piece) for at in places]
+            merged += jnp.dot(
+                rows[0] if len(rows) == 1 else jnp.concatenate(rows, axis=0),
+                w_all[p * piece : (p + 1) * piece, :],
+                preferred_element_type=jnp.float32,
+            )
         q = merged[:, :head_size]
         k = merged[:, head_size : 2 * head_size]
         v = merged[:, 2 * head_size :].astype(jnp.bfloat16)
@@ -200,27 +228,34 @@
             keys[there, :] = k[here]
             vals[there, :] = v[here]
 
-    project([z])
-
-    def hop(h, carry):
-        for e in (0, *PEERS):
-            for way in range(2):
-                z_wait(way, h - 1, e)
-                if far(way, e):
-                    z_copy(way, h, e).start()
-                else:
-
-                    @pl.when(h < 3)
-                    def _():
-                        z_copy(way, h, e).start()
-
-        project([z_at(-h), z_at(h)])
-        return carry
-
-    lax.fori_loop(1, 4, hop, 0)
-    for e in (0, *PEERS):
-        z_wait(e % 2, 3, e)
-    project([z_at(4)])
+    left = [sum(hops == h for _, _, hops, _ in ARRIVALS) for h in range(5)]
+    for e, p, h, way in ARRIVALS:
+        if h == 0:
+            y_wait(e, p)
+            for onward in range(2):
+                z_copy(onward, 0, e, p).start()
+            if p == 0:
+                y_copy(e, 0).wait_send()
+                y_copy(e, 1).start()
+        else:
+            z_wait(way, h - 1, e, p)
+            if h < reach(way, e):
+                z_copy(way, h, e, p).start()
+        left[h] -= 1
+        if left[h]:
+            continue
+        if h == 0:
+            for peer in PEERS:
+                w_copy(peer).start()
+            for peer in PEERS:
+                hid_copy(peer).start()
+            for j in range(3):
+                local[j].wait()
+            project([z])
+        elif h == 4:
+            project([z_at(4)])
+        else:
+            project([z_at(-h), z_at(h)])
 
     def head_copy(i, e):
         mine = heads.at[z_at(ORDER[i]), y]
@@ -255,7 +290,28 @@
         )
 
     def length(way, part):
-        return 4 if way == part else 3
+        return 4 if way == part % 2 else 3
+
+    def out_copy(yy):
+        return remote(
+            out_rows.at[yy],
+            out.at[:, my_cols],
+            out_send.at[yy],
+            out_recv.at[y],
+            yy,
+            z,
+            after,
+        )
+
+    gate = mod[2, :, my_cols]
+
+    def layer_rows(part, total):
+        for way in range(2):
+            ring_copy(way, part, 1).wait_recv()
+            total += part_in[way, part, 0].astype(jnp.float32)
+        layer_out = hid_cols[part].astype(jnp.float32) + gate * total
+        out_rows[part] = layer_out.astype(jnp.bfloat16)
+        out_copy(part).start()
 
     def finish(i):
         offset = ORDER[i]
@@ -271,28 +327,26 @@
             w_cols[...].reshape(NY * head_size, cols),
             preferred_element_type=jnp.float32,
         )
-        pieces = [summed[:half], summed[half:]]
+        pieces = [summed[part * own : (part + 1) * own] for part in range(NY)]
         k = abs(offset)
-        ways = (0, 1) if k in (0, 4) else ((0,) if offset > 0 else (1,))
+        if k == 0:
+            for part in range(NY):
+                layer_rows(part, pieces[part])
+            return
+        ways = (0, 1) if k == 4 else ((0,) if offset > 0 else (1,))
         for way in ways:
-            for part in range(2):
+            for part in (1 - way, 3 - way, way, 2 + way):
                 if k > length(way, part):
                     continue
+                added = pieces[part]
                 if k < length(way, part):
                     ring_copy(way, part, k + 1).wait_recv()
-                    added = pieces[part] + part_in[way, part, k].astype(jnp.float32)
-                else:
-                    added = pieces[part]
-                if k > 0:
-                    part_out[way, part, k - 1] = added.astype(jnp.bfloat16)
-                    ring_copy(way, part, k).start()
-                else:
-                    pieces[part] = added
-        return pieces
+                    added += part_in[way, part, k].astype(jnp.float32)
+                part_out[way, part, k - 1] = added.astype(jnp.bfloat16)
+                ring_copy(way, part, k).start()
 
     blocks = len(ORDER)
     ahead = 2
-    pieces = None
     for i in range(blocks + ahead):
         if i < blocks:
             attend(i)
@@ -306,39 +360,22 @@
                 ).wait_recv()
             local[4].wait()
         if i >= ahead:
-            pieces = finish(i - ahead)
-
-    def out_copy(yy):
-        return remote(
-            out_rows.at[yy],
-            out.at[:, my_cols],
-            out_send.at[yy],
-            out_recv.at[y],
-            yy,
-            z,
-            after,
-        )
-
-    gate = mod[2:3, my_cols]
-    for yy in range(NY):
-        total = pieces[yy // 2][(yy % 2) * own : (yy % 2 + 1) * own]
-        layer_out = hid_cols[yy].astype(jnp.float32) + gate * total
-        out_rows[yy] = layer_out.astype(jnp.bfloat16)
-        out_copy(yy).start()
+            finish(i - ahead)
 
     for e in PEERS:
-        y_copy(e).wait_send()
+        y_copy(e, 1).wait_send()
         hid_copy(e).wait_send()
         w_copy(e).wait_send()
     for e in range(NY):
         for way in range(2):
-            for h in range(4 if far(way, e) else 3):
-                z_copy(way, h, e).wait_send()
+            for h in range(reach(way, e)):
+                for p in range(PARTS):
+                    z_copy(way, h, e, p).wait_send()
     for i in range(blocks):
         for e in PEERS:
             head_copy(i, e).wait_send()
     for way in range(2):
-        for part in range(2):
+        for part in range(NY):
             for k in range(1, length(way, part) + 1):
                 ring_copy(way, part, k).wait_send()
     for yy in range(NY):
@@ -358,16 +395,18 @@
     cols = width // NY
     bf16 = jnp.bfloat16
     dma = pltpu.SemaphoreType.DMA
-    vmem = pl.BlockSpec(memory_space=pltpu.VMEM)
     anywhere = pl.BlockSpec(memory_space=pl.ANY)
     smem = pl.BlockSpec(memory_space=pltpu.SMEM)
     received = pl.pallas_call(
         functools.partial(kernel, sections),
         out_shape=jax.ShapeDtypeStruct((own, width), bf16),
-        in_specs=[vmem, vmem, anywhere, vmem, anywhere, anywhere, smem],
-        out_specs=vmem,
+        in_specs=[anywhere] * 6 + [smem],
+        out_specs=anywhere,
         scratch_shapes=[
-            pltpu.VMEM((NZ, NY, own, width), bf16),
+            pltpu.VMEM((own, width), bf16),
+            pltpu.VMEM((3, 1, width), jnp.float32),
+            pltpu.VMEM((2, head_size), jnp.float32),
+            pltpu.VMEM((NZ, PARTS, NY, own, width // PARTS), bf16),
             pltpu.VMEM((width, 3 * head_size), bf16),
             pltpu.VMEM((NY, head_size, cols), bf16),
             pltpu.VMEM((2, clip, head_size), bf16),
@@ -375,32 +414,32 @@
             pltpu.VMEM((clip, head_size), bf16),
             pltpu.VMEM((NZ, block, head_size), bf16),
             pltpu.VMEM((NZ, NY, block, head_size), bf16),
-            pltpu.VMEM((2, 2, 4, block // 2, cols), bf16),
-            pltpu.VMEM((2, 2, 4, block // 2, cols), bf16),
+            pltpu.VMEM((2, NY, 4, own, cols), bf16),
+            pltpu.VMEM((2, NY, 4, own, cols), bf16),
             pltpu.VMEM((NY, own, cols), bf16),
             pltpu.VMEM((NY, own, cols), bf16),
-            dma((5,)),
-            dma((NY,)),
-            dma((NY,)),
-            dma((NY,)),
-            dma((NY,)),
-            dma((NY,)),
-            dma((NY,)),
-            dma((2, 4, NY)),
-            dma((2, 4, NY)),
+            dma((8,)),
+            dma((NY, PARTS)),
+            dma((NY, PARTS)),
+            dma((NY,)),
+            dma((NY,)),
+            dma((NY,)),
+            dma((NY,)),
+            dma((2, 4, NY, PARTS)),
+            dma((2, 4, NY, PARTS)),
             dma((NZ, NY)),
             dma((NZ, NY)),
-            dma((2, 2, 4)),
-            dma((2, 2, 4)),
+            dma((2, NY, 4)),
+            dma((2, NY, 4)),
             dma((NY,)),
             dma((NY,)),
         ],
         compiler_params=pltpu.CompilerParams(
-            collective_id=0, has_side_effects=True, vmem_limit_bytes=48 << 20
+            collective_id=0, has_side_effects=True, vmem_limit_bytes=60 << 20
         ),
     )(
         hidden[0],
-        modulation[0],
+        jnp.transpose(modulation, (1, 0, 2)),
         jnp.transpose(w_qkv[0], (1, 0, 2)),
         qk_gain[0],
         w_out[0],

time: 103 us -> 87.9 us (0.85)
  the two profiles are of different devices: /device:TPU:3 before, /device:TPU:1 now
where the time goes in v2:
time: 87.9 us; the launch traced here: 87.8 us
  Pallas kernels  85.5 us (97%)
  local copies, waits for them, and re-layouts  1.57 us (2%)
    pallas_call x1, Pallas kernels, per_device(): pl.pallas_call(functools.partial(kernel, sections), out_shape=jax.ShapeDt...  85.5 us

profile of v2, /device:TPU:1, one launch (start us, length us, event | category | flops | bytes accessed | tf_op | source)
XLA Modules:
  0.0 87.8 jit_solution(1722656358776554486)
XLA Ops:
  0.7 85.5 %shard_map.73 = bf16[16,4096]{1,0:T(8,128)(2,1)} custom-call(bf16[16,4096]{1,0:T(8,128)(2,1)} %bitcast.13, f32[3,1,4096]{2,1,0:T(1,128)} %bitcast.14, bf16[3,4096,128]{2,1,0:T(8,128)(2,1)} %bitcast.9, f32[2,128]{1,0:T(2,128)} %bitcast.15, bf16[128,4096]{1,0:T(8,128)(2,1)} %bitcast.10, bf16[2,1024,128]{2,1,0:T(8,128)(2,1)} %bitcast.11, s32[1]{0:T(128)S(6)} %copy.9.start), custom_call_target="tpu_custom_call" | custom-call | tf_op jit(solution)/shard_map/pallas_call | solution.py:400
  86.2 1.6 %copy.10 = bf16[1,16,4096]{2,1,0:T(8,128)(2,1)} copy(bf16[1,16,4096]{2,1,0:T(8,128)(2,1)} %bitcast.12) | data formatting | bytes 262144

commit v3 on v2

--- a/solution.py
+++ b/solution.py
@@ -125,7 +125,7 @@
 
     barrier = pltpu.get_barrier_semaphore()
     partners = [(section, y_at(e) * NZ + z) for e in PEERS]
-    partners += [(section, y * NZ + z_at(s)) for s in (1, -1)]
+    partners += [(section, y * NZ + z_at(s)) for s in (1, -1, 2, -2)]
     partners += [(after, yy * NZ + z) for yy in range(NY)]
     partners += [(before, yy * NZ + z) for yy in range(NY)]
     for partner in partners:
@@ -286,7 +286,7 @@
             ring_send.at[way, part, k - 1],
             ring_recv.at[way, part, k - 1],
             y,
-            z_at(1 - 2 * way),
+            z_at((1 - 2 * way) * (2 if k == 4 else 1)),
         )
 
     def length(way, part):
@@ -335,18 +335,21 @@
             return
         ways = (0, 1) if k == 4 else ((0,) if offset > 0 else (1,))
         for way in ways:
-            for part in (1 - way, 3 - way, way, 2 + way):
+            for part in range(NY):
                 if k > length(way, part):
                     continue
                 added = pieces[part]
-                if k < length(way, part):
-                    ring_copy(way, part, k + 1).wait_recv()
-                    added += part_in[way, part, k].astype(jnp.float32)
+                came = [k + 1] if k < 3 else []
+                if k == 2 and length(way, part) == 4:
+                    came.append(4)
+                for c in came:
+                    ring_copy(way, part, c).wait_recv()
+                    added += part_in[way, part, c - 1].astype(jnp.float32)
                 part_out[way, part, k - 1] = added.astype(jnp.bfloat16)
                 ring_copy(way, part, k).start()
 
     blocks = len(ORDER)
-    ahead = 2
+    ahead = 3
     for i in range(blocks + ahead):
         if i < blocks:
             attend(i)

time: 87.9 us -> 86 us (0.978)
  Pallas kernels: 85.5 us -> 83.6 us
    pallas_call x1, Pallas kernels: 85.5 us -> 83.6 us  [per_device(): pl.pallas_call(functools.partial(kernel, sections), out_shape=jax.ShapeDt...]
where the time goes in v3:
time: 86 us; the launch traced here: 85.9 us
  Pallas kernels  83.6 us (97%)
  local copies, waits for them, and re-layouts  1.57 us (2%)
    pallas_call x1, Pallas kernels, per_device(): pl.pallas_call(functools.partial(kernel, sections), out_shape=jax.ShapeDt...  83.6 us

profile of v3, /device:TPU:1, one launch (start us, length us, event | category | flops | bytes accessed | tf_op | source)
XLA Modules:
  0.0 85.9 jit_solution(14240861365347094554)
XLA Ops:
  0.7 83.6 %shard_map.73 = bf16[16,4096]{1,0:T(8,128)(2,1)} custom-call(bf16[16,4096]{1,0:T(8,128)(2,1)} %bitcast.13, f32[3,1,4096]{2,1,0:T(1,128)} %bitcast.14, bf16[3,4096,128]{2,1,0:T(8,128)(2,1)} %bitcast.9, f32[2,128]{1,0:T(2,128)} %bitcast.15, bf16[128,4096]{1,0:T(8,128)(2,1)} %bitcast.10, bf16[2,1024,128]{2,1,0:T(8,128)(2,1)} %bitcast.11, s32[1]{0:T(128)S(6)} %copy.9.start), custom_call_target="tpu_custom_call" | custom-call | tf_op jit(solution)/shard_map/pallas_call | solution.py:403
  84.3 1.6 %copy.10 = bf16[1,16,4096]{2,1,0:T(8,128)(2,1)} copy(bf16[1,16,4096]{2,1,0:T(8,128)(2,1)} %bitcast.12) | data formatting | bytes 262144

commit v4 on v3

--- a/solution.py
+++ b/solution.py
@@ -398,13 +398,14 @@
     cols = width // NY
     bf16 = jnp.bfloat16
     dma = pltpu.SemaphoreType.DMA
-    anywhere = pl.BlockSpec(memory_space=pl.ANY)
+    hbm = pl.BlockSpec(memory_space=pltpu.HBM)
+    vmem = pl.BlockSpec(memory_space=pltpu.VMEM)
     smem = pl.BlockSpec(memory_space=pltpu.SMEM)
     received = pl.pallas_call(
         functools.partial(kernel, sections),
         out_shape=jax.ShapeDtypeStruct((own, width), bf16),
-        in_specs=[anywhere] * 6 + [smem],
-        out_specs=anywhere,
+        in_specs=[hbm] * 6 + [smem],
+        out_specs=vmem,
         scratch_shapes=[
             pltpu.VMEM((own, width), bf16),
             pltpu.VMEM((3, 1, width), jnp.float32),
@@ -438,15 +439,20 @@
             dma((NY,)),
         ],
         compiler_params=pltpu.CompilerParams(
-            collective_id=0, has_side_effects=True, vmem_limit_bytes=60 << 20
+            collective_id=0, has_side_effects=True, vmem_limit_bytes=48 << 20
         ),
     )(
-        hidden[0],
-        jnp.transpose(modulation, (1, 0, 2)),
-        jnp.transpose(w_qkv[0], (1, 0, 2)),
-        qk_gain[0],
-        w_out[0],
-        stale_kv[0],
+        *[
+            pltpu.with_memory_space_constraint(operand, pltpu.HBM)
+            for operand in (
+                hidden[0],
+                jnp.transpose(modulation, (1, 0, 2)),
+                jnp.transpose(w_qkv[0], (1, 0, 2)),
+                qk_gain[0],
+                w_out[0],
+                stale_kv[0],
+            )
+        ],
         patch_start,
     )
     return received[None]

time: 86 us -> 85 us (0.988)
  local copies, waits for them, and re-layouts: 1.57 us -> 0.66 us
    unnamed x1, local copies, waits for them, and re-layouts: 1.57 us -> 0.66 us
where the time goes in v4:
time: 85 us; the launch traced here: 84.8 us
  Pallas kernels  83.5 us (98%)
    pallas_call x1, Pallas kernels, per_device(): pl.pallas_call(functools.partial(kernel, sections), out_shape=jax.ShapeDt...  83.5 us

profile of v4, /device:TPU:1, one launch (start us, length us, event | category | flops | bytes accessed | tf_op | source)
XLA Modules:
  0.0 84.8 jit_solution(15167410054500288804)
XLA Ops:
  0.7 83.5 %shard_map.73 = bf16[16,4096]{1,0:T(8,128)(2,1)S(1)} custom-call(bf16[16,4096]{1,0:T(8,128)(2,1)} %bitcast.13, f32[3,1,4096]{2,1,0:T(1,128)} %bitcast.14, bf16[3,4096,128]{2,1,0:T(8,128)(2,1)} %bitcast.10, f32[2,128]{1,0:T(2,128)} %bitcast.15, bf16[128,4096]{1,0:T(8,128)(2,1)} %bitcast.11, bf16[2,1024,128]{2,1,0:T(8,128)(2,1)} %bitcast.12, s32[1]{0:T(128)S(6)} %copy.9.start), custom_call_target="tpu_custom_call" | custom-call | tf_op jit(solution)/shard_map/pallas_call | solution.py:404
  84.2 0.7 copy.10

commit v5 on v4

--- a/solution.py
+++ b/solution.py
@@ -205,15 +205,18 @@
         )
     query_scale = math.log2(math.e) / math.sqrt(head_size)
 
-    def project(places):
-        merged = 0.0
-        for p in range(PARTS):
-            rows = [rows_all[at, p].reshape(block, piece) for at in places]
-            merged += jnp.dot(
-                rows[0] if len(rows) == 1 else jnp.concatenate(rows, axis=0),
-                w_all[p * piece : (p + 1) * piece, :],
-                preferred_element_type=jnp.float32,
-            )
+    def product(places, p):
+        rows = [rows_all[at, p].reshape(block, piece) for at in places]
+        return jnp.dot(
+            rows[0] if len(rows) == 1 else jnp.concatenate(rows, axis=0),
+            w_all[p * piece : (p + 1) * piece, :],
+            preferred_element_type=jnp.float32,
+        )
+
+    def project(places, merged=None):
+        if merged is None:
+            merged = product(places, 0)
+        merged += product(places, 1)
         q = merged[:, :head_size]
         k = merged[:, head_size : 2 * head_size]
         v = merged[:, 2 * head_size :].astype(jnp.bfloat16)
@@ -229,6 +232,7 @@
             vals[there, :] = v[here]
 
     left = [sum(hops == h for _, _, hops, _ in ARRIVALS) for h in range(5)]
+    last_firsts = sum((p, hops) == (0, 4) for _, p, hops, _ in ARRIVALS)
     for e, p, h, way in ARRIVALS:
         if h == 0:
             y_wait(e, p)
@@ -242,6 +246,10 @@
             if h < reach(way, e):
                 z_copy(way, h, e, p).start()
         left[h] -= 1
+        if h == 4 and p == 0:
+            last_firsts -= 1
+            if not last_firsts:
+                early = product([z_at(4)], 0)
         if left[h]:
             continue
         if h == 0:
@@ -249,11 +257,12 @@
                 w_copy(peer).start()
             for peer in PEERS:
                 hid_copy(peer).start()
+        elif h == 4:
+            project([z_at(4)], early)
+        elif h == 1:
             for j in range(3):
                 local[j].wait()
-            project([z])
-        elif h == 4:
-            project([z_at(4)])
+            project([z, z_at(-h), z_at(h)])
         else:
             project([z_at(-h), z_at(h)])
 

time: 85 us -> 85 us (level)
  no operation moved by 1% of the time
where the time goes in v5:
time: 85 us; the launch traced here: 84.9 us
  Pallas kernels  83.6 us (98%)
    pallas_call x1, Pallas kernels, per_device(): pl.pallas_call(functools.partial(kernel, sections), out_shape=jax.ShapeDt...  83.6 us

profile of v5, /device:TPU:1, one launch (start us, length us, event | category | flops | bytes accessed | tf_op | source)
XLA Modules:
  0.0 84.9 jit_solution(4318754685775617629)
XLA Ops:
  0.7 83.6 %shard_map.73 = bf16[16,4096]{1,0:T(8,128)(2,1)S(1)} custom-call(bf16[16,4096]{1,0:T(8,128)(2,1)} %bitcast.13, f32[3,1,4096]{2,1,0:T(1,128)} %bitcast.14, bf16[3,4096,128]{2,1,0:T(8,128)(2,1)} %bitcast.10, f32[2,128]{1,0:T(2,128)} %bitcast.15, bf16[128,4096]{1,0:T(8,128)(2,1)} %bitcast.11, bf16[2,1024,128]{2,1,0:T(8,128)(2,1)} %bitcast.12, s32[1]{0:T(128)S(6)} %copy.9.start), custom_call_target="tpu_custom_call" | custom-call | tf_op jit(solution)/shard_map/pallas_call | solution.py:413
  84.2 0.7 copy.10
